TPU v7x, 256 devices: a whole 4x4x8 slice. The times are simulated.
256 devices in a mesh: leaf: 32 (over y, x, core), front: 8 (over z).
Axes of the slice: x: 4, y: 4, z: 8, core: 2. Of those that a mesh axis runs over, the one named last changes fastest.
Arguments:
- leaf_contrib: float32 [32768, 1024], P(('leaf', 'front')), may hold values from -1 to 7, as said below
- entries_lower: float32 [32768, 1024], P(('leaf', 'front')), may hold values from -1 to 4, as said below
- entries_middle: float32 [16384, 1024], P(('leaf', 'front')), may hold values from -1 to 4, as said below
- entries_upper: float32 [8192, 1024], P(('leaf', 'front')), may hold values from -1 to 4, as said below
- assembly_lower: int32 [16, 2, 8], replicated, may hold values from 0 to 15, as said below
- assembly_middle: int32 [8, 2, 8], replicated, may hold values from 0 to 15, as said below
- assembly_upper: int32 [4, 2, 8], replicated, may hold values from 0 to 15, as said below
Outputs:
- factor_lower: float32 [32768, 1024], P(('leaf', 'front'))
- factor_middle: float32 [16384, 1024], P(('leaf', 'front'))
- factor_upper: float32 [8192, 1024], P(('leaf', 'front'))
- top_update: float32 [4096, 1024], P(('leaf', 'front'))
Inputs may be any that keep to these rules, and one draw needn't show every extreme that they name: `leaf_contrib`: in natural row order each leaf's block is symmetric positive definite. `entries_lower`: in natural row order the first 1024 rows of each front's entries form a symmetric positive definite block. `entries_middle`: in natural row order the first 1024 rows of each front's entries form a symmetric positive definite block. `entries_upper`: in natural row order the first 1024 rows of each front's entries form a symmetric positive definite block. `assembly_lower`: each child's block j goes to parent block j or j + 8, and at least one of the two children sends its block j to j + 8. `assembly_middle`: each child's block j goes to parent block j or j + 8, and at least one of the two children sends its block j to j + 8. `assembly_upper`: each child's block j goes to parent block j or j + 8, and at least one of the two children sends its block j to j + 8.
All inputs are finite; a program needn't handle non-finite values.
Results may differ from a plain program's by a relative error of at most 0.0003.
Values sent between devices are 32-bit elements; how exact they have to be, the bound alone decides.
A program may use at most 128 MiB of HBM per device.

v0:
```python
import jax
import jax.numpy as jnp
from jax import lax
from jax.sharding import PartitionSpec as P

BLK = 128
PIVOT_BLOCKS = 8


def partner_2(value, axis, stride):
    mask = 2**stride
    pairs = [(source, source ^ mask) for source in range(lax.axis_size(axis))]
    return lax.ppermute(value, axis, pairs)


def product(left, right):
    return jnp.dot(left, right, precision=lax.Precision.HIGHEST, preferred_element_type=jnp.float32)


def factor_inverse(matrix):
    order_size = matrix.shape[0]
    if order_size <= 128 or order_size % 2 != 0:
        lower_factor = jnp.linalg.cholesky(matrix)
        identity = jnp.eye(order_size, dtype=jnp.float32)
        inverse = jax.scipy.linalg.solve_triangular(lower_factor, identity, lower=True)
        return (lower_factor, inverse)
    half = order_size // 2
    first_factor, first_inverse = factor_inverse(matrix[:half, :half])
    coupling = product(matrix[half:, :half], first_inverse.T)
    second_factor, second_inverse = factor_inverse(
        matrix[half:, half:] - product(coupling, coupling.T)
    )
    corner = -product(second_inverse, product(coupling, first_inverse))
    zeros_block = jnp.zeros((half, half), jnp.float32)
    lower_factor = jnp.concatenate(
        [
            jnp.concatenate([first_factor, zeros_block], 1),
            jnp.concatenate([coupling, second_factor], 1),
        ],
        0,
    )
    inverse = jnp.concatenate(
        [
            jnp.concatenate([first_inverse, zeros_block], 1),
            jnp.concatenate([corner, second_inverse], 1),
        ],
        0,
    )
    return (lower_factor, inverse)


def reversed_bits(number, bit_count):
    result = jnp.zeros((), jnp.int32)
    for bit_index in range(bit_count):
        result = result + (number >> bit_index & 1) * (1 << bit_count - 1 - bit_index)
    return result


def join_pieces(mine, theirs, bit_index, axis_index):
    upper_bit = lax.axis_index("leaf") >> bit_index & 1
    return jnp.where(
        upper_bit == 0,
        jnp.concatenate([mine, theirs], axis_index),
        jnp.concatenate([theirs, mine], axis_index),
    )


def group_gather(pieces, height):
    gathered = lax.all_gather(pieces[:, None], "front", axis=1, tiled=True)
    for bit_index in reversed(range(height)):
        partner = partner_2(gathered, "leaf", bit_index)
        gathered = join_pieces(gathered, partner, bit_index, 2)
    return gathered


def spread_columns(rows_in, upper_mask):
    blocks = rows_in.reshape(rows_in.shape[0], rows_in.shape[1], upper_mask.shape[0], -1)
    to_pivot = blocks * (1.0 - upper_mask)[None, None, :, None]
    to_update = blocks * upper_mask[None, None, :, None]
    return jnp.concatenate([to_pivot, to_update], axis=2).reshape(
        rows_in.shape[0], rows_in.shape[1], -1
    )


def own_rows(whole, front_index, piece_index, piece_rows):
    chosen = lax.dynamic_index_in_dim(whole, front_index, 1, keepdims=False)
    return lax.dynamic_slice_in_dim(chosen, piece_index * piece_rows, piece_rows, 1)


def local(
    leaf_contrib,
    entries_lower,
    entries_middle,
    entries_upper,
    assembly_lower,
    assembly_middle,
    assembly_upper,
):
    front_count = lax.axis_size("front")
    local_count = PIVOT_BLOCKS // front_count
    leaf_index = lax.axis_index("leaf")
    front_index = lax.axis_index("front")
    pivot_size = leaf_contrib.shape[1]
    update = leaf_contrib.reshape(local_count, BLK, pivot_size)
    my_blocks = front_index + front_count * jnp.arange(local_count, dtype=jnp.int32)
    selector = (jnp.arange(PIVOT_BLOCKS, dtype=jnp.int32)[None, :] == my_blocks[:, None]).astype(
        jnp.float32
    )
    results = []
    for height, entries, routes in (
        (1, entries_lower, assembly_lower),
        (2, entries_middle, assembly_middle),
        (3, entries_upper, assembly_upper),
    ):
        piece_rows = BLK // 2**height
        child_bit = leaf_index >> height - 1 & 1
        low_rows = update[:, :piece_rows]
        high_rows = update[:, piece_rows:]
        kept = jnp.where(child_bit == 0, low_rows, high_rows)
        outgoing = jnp.where(child_bit == 0, high_rows, low_rows)
        received = partner_2(outgoing, "leaf", height - 1)
        route_pair = lax.dynamic_index_in_dim(routes, leaf_index >> height, 0, keepdims=False)
        upper_masks = (route_pair >= PIVOT_BLOCKS).astype(jnp.float32)
        own_mask = jnp.where(child_bit == 0, upper_masks[0], upper_masks[1])
        other_mask = jnp.where(child_bit == 0, upper_masks[1], upper_masks[0])
        slab_rows = local_count * piece_rows
        pivot_slab = entries[:slab_rows].reshape(local_count, piece_rows, pivot_size)
        update_slab = jnp.zeros((local_count, piece_rows, 2 * pivot_size), jnp.float32)
        update_slab = update_slab.at[:, :, :pivot_size].set(
            entries[slab_rows:].reshape(local_count, piece_rows, pivot_size)
        )
        for contribution, column_mask in ((kept, own_mask), (received, other_mask)):
            spread = spread_columns(contribution, column_mask)
            row_upper = jnp.sum(selector * column_mask[None, :], axis=1)
            pivot_slab = pivot_slab + (1.0 - row_upper)[:, None, None] * spread[:, :, :pivot_size]
            update_slab = update_slab + row_upper[:, None, None] * spread
        piece_index = reversed_bits(leaf_index & 2**height - 1, height)
        update_pivot = update_slab[:, :, :pivot_size]
        whole_pivot = group_gather(pivot_slab, height).reshape(pivot_size, pivot_size)
        lower_factor, factor_inv = factor_inverse(whole_pivot)
        own_panel = product(update_pivot.reshape(-1, pivot_size), factor_inv.T)
        all_panel = group_gather(
            own_panel.reshape(local_count, piece_rows, pivot_size), height
        ).reshape(pivot_size, pivot_size)
        own_factor = own_rows(
            lower_factor.reshape(local_count, front_count, BLK, pivot_size),
            front_index,
            piece_index,
            piece_rows,
        ).reshape(-1, pivot_size)
        results.append(jnp.concatenate([own_factor, own_panel], axis=0))
        schur_rows = update_slab[:, :, pivot_size:].reshape(-1, pivot_size) - product(
            own_panel, all_panel.T
        )
        update = schur_rows.reshape(local_count, piece_rows, pivot_size)
    return (results[0], results[1], results[2], update.reshape(-1, pivot_size))


def solution(mesh):
    in_specs = (
        P(("leaf", "front"), None),
        P(("leaf", "front"), None),
        P(("leaf", "front"), None),
        P(("leaf", "front"), None),
        P(),
        P(),
        P(),
    )
    out_specs = (
        P(("leaf", "front"), None),
        P(("leaf", "front"), None),
        P(("leaf", "front"), None),
        P(("leaf", "front"), None),
    )
    return jax.shard_map(local, mesh=mesh, in_specs=in_specs, out_specs=out_specs, check_vma=False)
```

profile of v0, /device:TPU:1, one launch (start us, length us, event | category | flops | bytes accessed | tf_op | source)
XLA Modules:
  0.0 1222.6 jit_solution(8824010916489031496)
XLA Ops:
  16.0 38.2 %all-gather.11.cloned.1.call-done = f32[8,64,1024]{2,1,0:T(8,128)} async-done(((f32[1,64,1024]{2,1,0:T(8,128)}), f32[8,64,1024]{2,1,0:T(8,128)}) %all-gather.11.cloned.1.call-update) | async-done | bytes 2097168 | tf_op jit(solution)/shard_map/all_gather | solution.py:69
  68.6 11.7 cholesky.374
  95.2 11.7 cholesky.385
  122.0 11.7 cholesky.396
  148.6 11.9 cholesky.407
  180.1 12.1 cholesky.418
  205.2 11.7 cholesky.429
  230.5 11.9 cholesky.440
  265.1 12.1 cholesky.451
  307.0 35.7 %all-gather.13.cloned.1.call-done = f32[512,1024]{1,0:T(8,128)} async-done(((f32[64,1024]{1,0:T(8,128)}), f32[512,1024]{1,0:T(8,128)}) %all-gather.13.cloned.1.call-update) | async-done | bytes 2097168 | tf_op jit(solution)/shard_map/all_gather | solution.py:69
  364.3 32.8 %all-gather.15.cloned.1.call-done = f32[8,32,1024]{2,1,0:T(8,128)} async-done(((f32[1,32,1024]{2,1,0:T(8,128)}), f32[8,32,1024]{2,1,0:T(8,128)}) %all-gather.15.cloned.1.call-update) | async-done | bytes 1048592 | tf_op jit(solution)/shard_map/all_gather | solution.py:69
  398.3 17.9 %collective-permute-done.4 = f32[1,8,32,1024]{3,2,1,0:T(8,128)S(1)} collective-permute-done((f32[1,8,32,1024]{3,2,1,0:T(8,128)}, f32[1,8,32,1024]{3,2,1,0:T(8,128)S(1)}, u32[]{:S(2)}, u32[]{:S(2)}) %collective-permute-start.4) | collective-permute-done | bytes 1048608 | tf_op jit(solution)/shard_map/ppermute | solution.py:13
  432.5 11.7 cholesky.462
  459.2 11.7 cholesky.473
  486.0 11.7 cholesky.484
  513.6 12.1 cholesky.495
  548.5 11.9 cholesky.506
  575.0 11.7 cholesky.517
  606.6 13.6 %cholesky.528 = f32[128,128]{1,0:T(8,128)} custom-call(f32[128,128]{1,0:T(8,128)} %fusion.248), custom_call_target="Cholesky" | custom-call | tf_op jit(solution)/shard_map/jit(cholesky)/cholesky | solution.py:23
  648.3 11.9 cholesky.539
  687.6 32.6 %all-gather.17.cloned.1.call-done = f32[256,1024]{1,0:T(8,128)} async-done(((f32[32,1024]{1,0:T(8,128)}), f32[256,1024]{1,0:T(8,128)}) %all-gather.17.cloned.1.call-update) | async-done | bytes 1048592 | tf_op jit(solution)/shard_map/all_gather | solution.py:69
  721.4 17.9 %collective-permute-done.6 = f32[1,8,32,1024]{3,2,1,0:T(8,128)S(1)} collective-permute-done((f32[1,8,32,1024]{3,2,1,0:T(8,128)}, f32[1,8,32,1024]{3,2,1,0:T(8,128)S(1)}, u32[]{:S(2)}, u32[]{:S(2)}) %collective-permute-start.6) | collective-permute-done | bytes 1048608 | tf_op jit(solution)/shard_map/ppermute | solution.py:13
  766.9 19.8 %all-gather.4 = f32[8,16,1024]{2,1,0:T(8,128)S(1)} all-gather(f32[1,16,1024]{2,1,0:T(8,128)S(1)} %get-tuple-element.121), channel_id=6, replica_groups=mesh['leaf'=32,'front'=8] {'front'}, dimensions={0}, use_global_device_ids=true | all-gather | bytes 589824 | tf_op jit(solution)/shard_map/all_gather | solution.py:69
  797.8 21.0 %collective-permute-done.10 = f32[1,8,32,1024]{3,2,1,0:T(8,128)S(1)} collective-permute-done((f32[1,8,32,1024]{3,2,1,0:T(8,128)S(1)}, f32[1,8,32,1024]{3,2,1,0:T(8,128)S(1)}, u32[]{:S(2)}, u32[]{:S(2)}) %collective-permute-start.10) | collective-permute-done | bytes 1048608 | tf_op jit(solution)/shard_map/ppermute | solution.py:13
  835.3 11.7 cholesky.550
  862.0 11.7 cholesky.561
  921.8 11.9 cholesky.583
  961.6 12.9 %cholesky.594 = f32[128,128]{1,0:T(8,128)S(1)} custom-call(f32[128,128]{1,0:T(8,128)} %fusion.236), custom_call_target="Cholesky" | custom-call | tf_op jit(solution)/shard_map/jit(cholesky)/cholesky | solution.py:23
  995.6 13.2 %cholesky.605 = f32[128,128]{1,0:T(8,128)} custom-call(f32[128,128]{1,0:T(8,128)} %fusion.234), custom_call_target="Cholesky" | custom-call | tf_op jit(solution)/shard_map/jit(cholesky)/cholesky | solution.py:23
  1036.8 13.3 %cholesky.616 = f32[128,128]{1,0:T(8,128)} custom-call(f32[128,128]{1,0:T(8,128)} %fusion.232), custom_call_target="Cholesky" | custom-call | tf_op jit(solution)/shard_map/jit(cholesky)/cholesky | solution.py:23
  1080.8 12.7 %cholesky.627 = f32[128,128]{1,0:T(8,128)S(1)} custom-call(f32[128,128]{1,0:T(8,128)} %fusion.230), custom_call_target="Cholesky" | custom-call | tf_op jit(solution)/shard_map/jit(cholesky)/cholesky | solution.py:23
  1123.5 21.8 %all-gather.5 = f32[128,1024]{1,0:T(8,128)} all-gather(f32[16,1024]{1,0:T(8,128)S(1)} %fusion), channel_id=7, replica_groups=mesh['leaf'=32,'front'=8] {'front'}, dimensions={0}, use_global_device_ids=true | all-gather | bytes 589824 | tf_op jit(solution)/shard_map/all_gather | solution.py:69
  (675 shorter events, 685.1 us)
Async XLA Ops:
  7.2 47.1 %all-gather.11.cloned.1.call-start = ((), (), s32[]{:S(2)}) async-start(), calls=%async_computation | async-start | bytes 2359296 | tf_op jit(solution)/shard_map/all_gather | solution.py:69
  8.3 6.4 collective-permute-start
  16.0 326.7 %all-gather.13.cloned.1.call-start = ((), (), s32[]{:S(2)}) async-start(), calls=%async_computation.1 | async-start | bytes 2359296 | tf_op jit(solution)/shard_map/all_gather | solution.py:69
  54.2 8.4 collective-permute-start.1
  119.6 54.9 %copy-start.53 = (f32[256,256]{1,0:T(8,128)}, f32[256,256]{1,0:T(8,128)S(1)}, u32[]{:S(2)}) copy-start(f32[256,256]{1,0:T(8,128)S(1)} %select_maximum_fusion.25) | copy-start | bytes 786436
  180.0 79.2 %copy-start.44 = (f32[128,256]{1,0:T(8,128)S(1)}, f32[128,256]{1,0:T(8,128)}, u32[]{:S(2)}) copy-start(f32[128,256]{1,0:T(8,128)} %copy-done.43) | copy-start | bytes 393220
  204.5 58.7 %copy-start.22 = (f32[128,128]{0,1:T(8,128)}, f32[128,128]{0,1:T(8,128)S(1)}, u32[]{:S(2)}) copy-start(f32[128,128]{0,1:T(8,128)S(1)} %fusion.223) | copy-start | bytes 196612
  229.8 60.9 %copy-start.5 = (f32[256,256]{0,1:T(8,128)}, f32[256,256]{0,1:T(8,128)S(1)}, u32[]{:S(2)}) copy-start(f32[256,256]{0,1:T(8,128)S(1)} %fusion.163) | copy-start | bytes 786436
  306.9 90.2 %all-gather.15.cloned.1.call-start = ((), (), s32[]{:S(2)}) async-start(), calls=%async_computation.2 | async-start | bytes 1179648 | tf_op jit(solution)/shard_map/all_gather | solution.py:69
  342.7 8.4 collective-permute-start.2
  358.4 4.8 collective-permute-start.3
  364.2 356.0 %all-gather.17.cloned.1.call-start = ((), (), s32[]{:S(2)}) async-start(), calls=%async_computation.3 | async-start | bytes 1179648 | tf_op jit(solution)/shard_map/all_gather | solution.py:69
  397.1 19.1 %collective-permute-start.4 = (f32[1,8,32,1024]{3,2,1,0:T(8,128)}, f32[1,8,32,1024]{3,2,1,0:T(8,128)S(1)}, u32[]{:S(2)}, u32[]{:S(2)}) collective-permute-start(f32[1,8,32,1024]{3,2,1,0:T(8,128)} %bitcast.535), channel_id=1, source_target_pairs={{0,16},{8,24},{16,0},{24,8},{32,48},{40,56},{48,32},{56,40},{64,80... | collective-permute-start | bytes 3145736 | tf_op jit(solution)/shard_map/ppermute | solution.py:13
  418.0 10.7 collective-permute-start.5
  457.4 56.1 %copy-start.24 = (f32[128,128]{0,1:T(8,128)}, f32[128,128]{0,1:T(8,128)S(1)}, u32[]{:S(2)}) copy-start(f32[128,128]{0,1:T(8,128)S(1)} %fusion.219) | copy-start | bytes 196612
  483.6 56.1 %copy-start.54 = (f32[256,256]{1,0:T(8,128)}, f32[256,256]{1,0:T(8,128)S(1)}, u32[]{:S(2)}) copy-start(f32[256,256]{1,0:T(8,128)S(1)} %select_maximum_fusion.21) | copy-start | bytes 786436
  485.0 53.5 %copy-start.6 = (f32[256,256]{0,1:T(8,128)}, f32[256,256]{0,1:T(8,128)S(1)}, u32[]{:S(2)}) copy-start(f32[256,256]{0,1:T(8,128)S(1)} %fusion.160) | copy-start | bytes 786436
  547.4 97.1 %copy-start.41 = (f32[128,256]{1,0:T(8,128)S(1)}, f32[128,256]{1,0:T(8,128)}, u32[]{:S(2)}) copy-start(f32[128,256]{1,0:T(8,128)} %copy-done.40) | copy-start | bytes 393220
  547.4 97.1 %copy-start.51 = (f32[256,256]{1,0:T(8,128)S(1)}, f32[256,256]{1,0:T(8,128)}, u32[]{:S(2)}) copy-start(f32[256,256]{1,0:T(8,128)} %copy-done.50) | copy-start | bytes 786436
  547.4 97.1 %copy-start.55 = (f32[256,256]{1,0:T(8,128)S(1)}, f32[256,256]{1,0:T(8,128)}, u32[]{:S(2)}) copy-start(f32[256,256]{1,0:T(8,128)} %copy-done.54) | copy-start | bytes 786436
  600.5 71.7 %copy-start.8 = (f32[256,256]{0,1:T(8,128)}, f32[256,256]{0,1:T(8,128)S(1)}, u32[]{:S(2)}) copy-start(f32[256,256]{0,1:T(8,128)S(1)} %fusion.158) | copy-start | bytes 786436
  720.2 19.1 %collective-permute-start.6 = (f32[1,8,32,1024]{3,2,1,0:T(8,128)}, f32[1,8,32,1024]{3,2,1,0:T(8,128)S(1)}, u32[]{:S(2)}, u32[]{:S(2)}) collective-permute-start(f32[1,8,32,1024]{3,2,1,0:T(8,128)} %bitcast.537), channel_id=1, source_target_pairs={{0,16},{8,24},{16,0},{24,8},{32,48},{40,56},{48,32},{56,40},{64,80... | collective-permute-start | bytes 3145736 | tf_op jit(solution)/shard_map/ppermute | solution.py:13
  742.6 10.8 collective-permute-start.7
  761.9 4.7 collective-permute-start.8
  786.7 9.5 collective-permute-start.9
  796.4 22.4 %collective-permute-start.10 = (f32[1,8,32,1024]{3,2,1,0:T(8,128)S(1)}, f32[1,8,32,1024]{3,2,1,0:T(8,128)S(1)}, u32[]{:S(2)}, u32[]{:S(2)}) collective-permute-start(f32[1,8,32,1024]{3,2,1,0:T(8,128)S(1)} %maximum_select_fusion.11), channel_id=1, source_target_pairs={{0,16},{8,24},{16,0},{24,8},{32,48},{40,56},{48,32},{56,40},{64,80... | collective-permute-start | bytes 3145736 | tf_op jit(solution)/shard_map/ppermute | solution.py:13
  819.0 12.4 %collective-permute-start.11 = (f32[1,8,64,1024]{3,2,1,0:T(8,128)S(1)}, f32[1,8,64,1024]{3,2,1,0:T(8,128)S(1)}, u32[]{:S(2)}, u32[]{:S(2)}) collective-permute-start(f32[1,8,64,1024]{3,2,1,0:T(8,128)S(1)} %maximum_select_fusion.8), channel_id=1, source_target_pairs={{0,8},{8,0},{16,24},{24,16},{32,40},{40,32},{48,56},{56,48},{64,72... | collective-permute-start | bytes 6291464 | tf_op jit(solution)/shard_map/ppermute | solution.py:13
  886.3 61.1 %copy-start.56 = (f32[256,256]{1,0:T(8,128)}, f32[256,256]{1,0:T(8,128)S(1)}, u32[]{:S(2)}) copy-start(f32[256,256]{1,0:T(8,128)S(1)} %select_maximum_fusion.17) | copy-start | bytes 786436
  887.8 59.7 %copy-start.10 = (f32[256,256]{0,1:T(8,128)}, f32[256,256]{0,1:T(8,128)S(1)}, u32[]{:S(2)}) copy-start(f32[256,256]{0,1:T(8,128)S(1)} %fusion.156) | copy-start | bytes 786436
  1145.3 13.5 %collective-permute-start.12 = (f32[1,8,16,1024]{3,2,1,0:T(8,128)}, f32[1,8,16,1024]{3,2,1,0:T(8,128)}, u32[]{:S(2)}, u32[]{:S(2)}) collective-permute-start(f32[1,8,16,1024]{3,2,1,0:T(8,128)} %bitcast.118), channel_id=1, source_target_pairs={{0,32},{8,40},{16,48},{24,56},{32,0},{40,8},{48,16},{56,24},{64,96... | collective-permute-start | bytes 1572872 | tf_op jit(solution)/shard_map/ppermute | solution.py:13
  1161.5 19.0 %collective-permute-start.13 = (f32[1,8,32,1024]{3,2,1,0:T(8,128)}, f32[1,8,32,1024]{3,2,1,0:T(8,128)}, u32[]{:S(2)}, u32[]{:S(2)}) collective-permute-start(f32[1,8,32,1024]{3,2,1,0:T(8,128)} %maximum_select_fusion.13), channel_id=1, source_target_pairs={{0,16},{8,24},{16,0},{24,8},{32,48},{40,56},{48,32},{56,40},{64,80... | collective-permute-start | bytes 3145736 | tf_op jit(solution)/shard_map/ppermute | solution.py:13
  1183.8 23.1 %collective-permute-start.14 = (f32[1,8,64,1024]{3,2,1,0:T(8,128)}, f32[1,8,64,1024]{3,2,1,0:T(8,128)}, u32[]{:S(2)}, u32[]{:S(2)}) collective-permute-start(f32[1,8,64,1024]{3,2,1,0:T(8,128)} %maximum_select_fusion.9), channel_id=1, source_target_pairs={{0,8},{8,0},{16,24},{24,16},{32,40},{40,32},{48,56},{56,48},{64,72... | collective-permute-start | bytes 6291464 | tf_op jit(solution)/shard_map/ppermute | solution.py:13
  (93 other events, 1117.1 us)
Sparse Core Ops, SparseCore 0:
  16.1 38.1 all-gather.10
  307.0 35.6 all-gather.12
  364.3 32.6 all-gather.14
  687.7 32.4 all-gather.16
where the time goes:
time: 1240 us; the launch traced here: 1220 us
  other arithmetic  675 us (54%)
  waiting for transfers between devices  223 us (18%)
  matrix products  145 us (12%)
  local copies, waits for them, and re-layouts  62.3 us (5%)
  starting transfers between devices  54.2 us (4%)
  blocking collectives  41.6 us (3%)
  between operations  21.2 us (2%)
    another operation x72, other arithmetic, factor_inverse(): lower_factor = jnp.linalg.cholesky(matrix)  309 us
    another operation x48, other arithmetic, factor_inverse(): jax.scipy.linalg.solve_triangular(lower_factor, identity, lower=True)  277 us
    all_gather x4, waiting for transfers between devices, group_gather(): gathered = lax.all_gather(pieces[:, None], 'front', axis=1, tiled=True)  139 us
    dot_general x90, matrix products, product(): jnp.dot(left, right, precision=lax.Precision.HIGHEST, preferred_element_t...  133 us
    ppermute x15, waiting for transfers between devices, partner_2(): return lax.ppermute(value, axis, pairs)  83.9 us
    ppermute x15, starting transfers between devices, partner_2(): return lax.ppermute(value, axis, pairs)  54 us
    all_gather x2, blocking collectives, group_gather(): gathered = lax.all_gather(pieces[:, None], 'front', axis=1, tiled=True)  41.6 us
    select_n x12, other arithmetic, join_pieces(): jnp.where(upper_bit == 0, jnp.concatenate([mine, theirs], axis_index), jn...  27.9 us
  transfers between devices with their start and end apart: 19, of which 16 were waited for; matrix products, arithmetic and copies ran while one was open for 4% of the time, Pallas kernels for 0%

commit v1 on v0

--- a/solution.py
+++ b/solution.py
@@ -66,7 +66,25 @@
 
 
 def group_gather(pieces, height):
-    gathered = lax.all_gather(pieces[:, None], "front", axis=1, tiled=True)
+    value_2 = pieces[:, None]
+    size, here, rows = (lax.axis_size("front"), lax.axis_index("front"), value_2.shape[1])
+    forward = [(i, (i + 1) % size) for i in range(size)]
+    behind = [(i, (i - 1) % size) for i in range(size)]
+    whole_2 = jnp.zeros((*value_2.shape[:1], size * rows, *value_2.shape[1 + 1 :]), value_2.dtype)
+    whole_2 = lax.dynamic_update_slice_in_dim(whole_2, value_2, here * rows, axis=1)
+    from_left = from_right = value_2
+    halfway = size // 2
+    for turn in range(1, halfway + 1):
+        from_left = lax.ppermute(from_left, "front", forward)
+        whole_2 = lax.dynamic_update_slice_in_dim(
+            whole_2, from_left, (here - turn) % size * rows, axis=1
+        )
+        if turn < size - halfway:
+            from_right = lax.ppermute(from_right, "front", behind)
+            whole_2 = lax.dynamic_update_slice_in_dim(
+                whole_2, from_right, (here + turn) % size * rows, axis=1
+            )
+    gathered = whole_2
     for bit_index in reversed(range(height)):
         partner = partner_2(gathered, "leaf", bit_index)
         gathered = join_pieces(gathered, partner, bit_index, 2)

time: 1240 us -> 1170 us (0.944)
  waiting for transfers between devices: 223 us -> 163 us
  starting transfers between devices: 54.2 us -> 102 us
  blocking collectives: 41.6 us -> 0 us
  between operations: 21.2 us -> 8.4 us
    all_gather x4 -> x0, waiting for transfers between devices: 139 us -> none  [group_gather(): gathered = lax.all_gather(pieces[:, None], 'front', axis=1, tiled=True)]
    ppermute x0 -> x42, waiting for transfers between devices: none -> 81.4 us  [the longest x24 80.5 us: group_gather(): from_left = lax.ppermute(from_left, 'front', forward)]
    ppermute x0 -> x42, starting transfers between devices: none -> 51.1 us  [the longest x18 50.3 us: group_gather(): from_right = lax.ppermute(from_right, 'front', behind)]
    all_gather x2 -> x0, blocking collectives: 41.6 us -> none  [group_gather(): gathered = lax.all_gather(pieces[:, None], 'front', axis=1, tiled=True)]
  transfers between devices with their start and end apart: 19 -> 57, of which waited for: 16 -> 37; matrix products, arithmetic and copies ran while one was open for 4% -> 5% of each run, Pallas kernels for 0% -> 0%
where the time goes in v1:
time: 1170 us; the launch traced here: 1160 us
  other arithmetic  674 us (58%)
  waiting for transfers between devices  163 us (14%)
  matrix products  142 us (12%)
  starting transfers between devices  102 us (9%)
  local copies, waits for them, and re-layouts  71.4 us (6%)
    another operation x72, other arithmetic, factor_inverse(): lower_factor = jnp.linalg.cholesky(matrix)  311 us
    another operation x48, other arithmetic, factor_inverse(): jax.scipy.linalg.solve_triangular(lower_factor, identity, lower=True)  277 us
    dot_general x90, matrix products, product(): jnp.dot(left, right, precision=lax.Precision.HIGHEST, preferred_element_t...  130 us
    ppermute x15, waiting for transfers between devices, partner_2(): return lax.ppermute(value, axis, pairs)  81.8 us
    ppermute x24, waiting for transfers between devices, group_gather(): from_left = lax.ppermute(from_left, 'front', forward)  80.5 us
    ppermute x15, starting transfers between devices, partner_2(): return lax.ppermute(value, axis, pairs)  50.9 us
    ppermute x18, starting transfers between devices, group_gather(): from_right = lax.ppermute(from_right, 'front', behind)  50.3 us
  transfers between devices with their start and end apart: 57, of which 37 were waited for; matrix products, arithmetic and copies ran while one was open for 5% of the time, Pallas kernels for 0%

profile of v1, /device:TPU:1, one launch (start us, length us, event | category | flops | bytes accessed | tf_op | source)
XLA Modules:
  0.0 1161.0 jit_solution(12407049360768904700)
XLA Ops:
  54.2 11.7 %cholesky.374 = f32[128,128]{1,0:T(8,128)S(1)} custom-call(f32[128,128]{1,0:T(8,128)S(1)} %get-tuple-element.113), custom_call_target="Cholesky" | custom-call | tf_op jit(solution)/shard_map/jit(cholesky)/cholesky | solution.py:23
  80.9 11.7 %cholesky.385 = f32[128,128]{1,0:T(8,128)S(1)} custom-call(f32[128,128]{1,0:T(8,128)S(1)} %fusion.277), custom_call_target="Cholesky" | custom-call | tf_op jit(solution)/shard_map/jit(cholesky)/cholesky | solution.py:23
  107.6 11.7 %cholesky.396 = f32[128,128]{1,0:T(8,128)S(1)} custom-call(f32[128,128]{1,0:T(8,128)S(1)} %fusion.275), custom_call_target="Cholesky" | custom-call | tf_op jit(solution)/shard_map/jit(cholesky)/cholesky | solution.py:23
  134.2 11.9 %cholesky.407 = f32[128,128]{1,0:T(8,128)S(1)} custom-call(f32[128,128]{1,0:T(8,128)S(1)} %fusion.273), custom_call_target="Cholesky" | custom-call | tf_op jit(solution)/shard_map/jit(cholesky)/cholesky | solution.py:23
  165.9 12.1 %cholesky.418 = f32[128,128]{1,0:T(8,128)S(1)} custom-call(f32[128,128]{1,0:T(8,128)S(1)} %fusion.271), custom_call_target="Cholesky" | custom-call | tf_op jit(solution)/shard_map/jit(cholesky)/cholesky | solution.py:23
  190.9 11.7 %cholesky.429 = f32[128,128]{1,0:T(8,128)S(1)} custom-call(f32[128,128]{1,0:T(8,128)S(1)} %fusion.269), custom_call_target="Cholesky" | custom-call | tf_op jit(solution)/shard_map/jit(cholesky)/cholesky | solution.py:23
  219.3 11.9 %cholesky.440 = f32[128,128]{1,0:T(8,128)S(1)} custom-call(f32[128,128]{1,0:T(8,128)S(1)} %fusion.267), custom_call_target="Cholesky" | custom-call | tf_op jit(solution)/shard_map/jit(cholesky)/cholesky | solution.py:23
  252.1 12.1 %cholesky.451 = f32[128,128]{1,0:T(8,128)S(1)} custom-call(f32[128,128]{1,0:T(8,128)S(1)} %fusion.265), custom_call_target="Cholesky" | custom-call | tf_op jit(solution)/shard_map/jit(cholesky)/cholesky | solution.py:23
  362.0 17.6 %collective-permute-done.25 = f32[1,8,32,1024]{3,2,1,0:T(8,128)S(1)} collective-permute-done((f32[1,8,32,1024]{3,2,1,0:T(8,128)S(1)}, f32[1,8,32,1024]{3,2,1,0:T(8,128)S(1)}, u32[]{:S(2)}, u32[]{:S(2)}) %collective-permute-start.25) | collective-permute-done | bytes 1048608 | tf_op jit(solution)/shard_map/ppermute | solution.py:13
  394.6 11.7 %cholesky.462 = f32[128,128]{1,0:T(8,128)S(1)} custom-call(f32[128,128]{1,0:T(8,128)S(1)} %get-tuple-element.111), custom_call_target="Cholesky" | custom-call | tf_op jit(solution)/shard_map/jit(cholesky)/cholesky | solution.py:23
  421.3 11.7 %cholesky.473 = f32[128,128]{1,0:T(8,128)S(1)} custom-call(f32[128,128]{1,0:T(8,128)S(1)} %fusion.261), custom_call_target="Cholesky" | custom-call | tf_op jit(solution)/shard_map/jit(cholesky)/cholesky | solution.py:23
  448.0 11.7 %cholesky.484 = f32[128,128]{1,0:T(8,128)S(1)} custom-call(f32[128,128]{1,0:T(8,128)S(1)} %fusion.259), custom_call_target="Cholesky" | custom-call | tf_op jit(solution)/shard_map/jit(cholesky)/cholesky | solution.py:23
  475.6 11.9 %cholesky.495 = f32[128,128]{1,0:T(8,128)S(1)} custom-call(f32[128,128]{1,0:T(8,128)S(1)} %fusion.257), custom_call_target="Cholesky" | custom-call | tf_op jit(solution)/shard_map/jit(cholesky)/cholesky | solution.py:23
  510.3 12.1 %cholesky.506 = f32[128,128]{1,0:T(8,128)S(1)} custom-call(f32[128,128]{1,0:T(8,128)S(1)} %fusion.255), custom_call_target="Cholesky" | custom-call | tf_op jit(solution)/shard_map/jit(cholesky)/cholesky | solution.py:23
  537.1 11.7 %cholesky.517 = f32[128,128]{1,0:T(8,128)S(1)} custom-call(f32[128,128]{1,0:T(8,128)S(1)} %fusion.253), custom_call_target="Cholesky" | custom-call | tf_op jit(solution)/shard_map/jit(cholesky)/cholesky | solution.py:23
  568.7 13.3 %cholesky.528 = f32[128,128]{1,0:T(8,128)} custom-call(f32[128,128]{1,0:T(8,128)} %fusion.251), custom_call_target="Cholesky" | custom-call | tf_op jit(solution)/shard_map/jit(cholesky)/cholesky | solution.py:23
  585.7 11.3 custom-call.42
  611.2 12.1 %cholesky.539 = f32[128,128]{1,0:T(8,128)S(1)} custom-call(f32[128,128]{1,0:T(8,128)S(1)} %fusion.249), custom_call_target="Cholesky" | custom-call | tf_op jit(solution)/shard_map/jit(cholesky)/cholesky | solution.py:23
  673.2 18.8 %collective-permute-done.34 = f32[1,8,32,1024]{3,2,1,0:T(8,128)S(1)} collective-permute-done((f32[1,8,32,1024]{3,2,1,0:T(8,128)S(1)}, f32[1,8,32,1024]{3,2,1,0:T(8,128)S(1)}, u32[]{:S(2)}, u32[]{:S(2)}) %collective-permute-start.34) | collective-permute-done | bytes 1048608 | tf_op jit(solution)/shard_map/ppermute | solution.py:13
  745.9 21.1 %collective-permute-done.45 = f32[1,8,32,1024]{3,2,1,0:T(8,128)S(1)} collective-permute-done((f32[1,8,32,1024]{3,2,1,0:T(8,128)S(1)}, f32[1,8,32,1024]{3,2,1,0:T(8,128)S(1)}, u32[]{:S(2)}, u32[]{:S(2)}) %collective-permute-start.45) | collective-permute-done | bytes 1048608 | tf_op jit(solution)/shard_map/ppermute | solution.py:13
  782.2 11.7 %cholesky.550 = f32[128,128]{1,0:T(8,128)S(1)} custom-call(f32[128,128]{1,0:T(8,128)S(1)} %get-tuple-element.109), custom_call_target="Cholesky" | custom-call | tf_op jit(solution)/shard_map/jit(cholesky)/cholesky | solution.py:23
  808.9 11.7 %cholesky.561 = f32[128,128]{1,0:T(8,128)S(1)} custom-call(f32[128,128]{1,0:T(8,128)S(1)} %fusion.245), custom_call_target="Cholesky" | custom-call | tf_op jit(solution)/shard_map/jit(cholesky)/cholesky | solution.py:23
  837.3 11.7 %cholesky.572 = f32[128,128]{1,0:T(8,128)S(1)} custom-call(f32[128,128]{1,0:T(8,128)S(1)} %fusion.243), custom_call_target="Cholesky" | custom-call | tf_op jit(solution)/shard_map/jit(cholesky)/cholesky | solution.py:23
  866.3 12.7 %cholesky.583 = f32[128,128]{1,0:T(8,128)S(1)} custom-call(f32[128,128]{1,0:T(8,128)} %fusion.241), custom_call_target="Cholesky" | custom-call | tf_op jit(solution)/shard_map/jit(cholesky)/cholesky | solution.py:23
  906.2 12.9 %cholesky.594 = f32[128,128]{1,0:T(8,128)S(1)} custom-call(f32[128,128]{1,0:T(8,128)} %fusion.239), custom_call_target="Cholesky" | custom-call | tf_op jit(solution)/shard_map/jit(cholesky)/cholesky | solution.py:23
  921.2 11.3 custom-call.48
  940.4 13.2 %cholesky.605 = f32[128,128]{1,0:T(8,128)} custom-call(f32[128,128]{1,0:T(8,128)} %fusion.237), custom_call_target="Cholesky" | custom-call | tf_op jit(solution)/shard_map/jit(cholesky)/cholesky | solution.py:23
  957.2 11.3 custom-call.49
  981.5 13.3 %cholesky.616 = f32[128,128]{1,0:T(8,128)} custom-call(f32[128,128]{1,0:T(8,128)} %fusion.235), custom_call_target="Cholesky" | custom-call | tf_op jit(solution)/shard_map/jit(cholesky)/cholesky | solution.py:23
  998.4 11.3 custom-call.50
  1025.5 13.4 %cholesky.627 = f32[128,128]{1,0:T(8,128)} custom-call(f32[128,128]{1,0:T(8,128)} %fusion.233), custom_call_target="Cholesky" | custom-call | tf_op jit(solution)/shard_map/jit(cholesky)/cholesky | solution.py:23
  1042.4 11.3 custom-call.51
  (806 shorter events, 747.0 us)
Async XLA Ops:
  1.7 5.7 collective-permute-start
  9.0 10.7 collective-permute-start.1
  9.1 10.6 collective-permute-start.2
  19.7 8.8 collective-permute-start.3
  19.7 10.7 collective-permute-start.4
  28.5 7.8 collective-permute-start.5
  30.5 6.6 collective-permute-start.6
  36.3 6.4 collective-permute-start.7
  42.7 7.9 collective-permute-start.8
  289.6 8.8 collective-permute-start.9
  289.7 8.7 collective-permute-start.10
  298.4 7.8 collective-permute-start.11
  298.4 7.9 collective-permute-start.12
  306.2 6.9 collective-permute-start.13
  306.3 6.9 collective-permute-start.14
  313.1 6.4 collective-permute-start.15
  319.6 8.2 collective-permute-start.16
  340.1 5.1 collective-permute-start.18
  340.2 5.0 collective-permute-start.19
  355.3 5.4 collective-permute-start.24
  360.6 18.9 %collective-permute-start.25 = (f32[1,8,32,1024]{3,2,1,0:T(8,128)S(1)}, f32[1,8,32,1024]{3,2,1,0:T(8,128)S(1)}, u32[]{:S(2)}, u32[]{:S(2)}) collective-permute-start(f32[1,8,32,1024]{3,2,1,0:T(8,128)S(1)} %constant_dynamic-update-slice_fusion.24), channel_id=1, source_target_pairs={{0,16},{8,24},{16,0},{24,8},{32,48},{40,56},{48,32},{56,40},{64,80... | collective-permute-start | bytes 3145736 | tf_op jit(solution)/shard_map/ppermute | solution.py:13
  379.8 11.0 collective-permute-start.26
  650.8 6.0 collective-permute-start.27
  650.9 5.9 collective-permute-start.28
  671.9 20.1 %collective-permute-start.34 = (f32[1,8,32,1024]{3,2,1,0:T(8,128)S(1)}, f32[1,8,32,1024]{3,2,1,0:T(8,128)S(1)}, u32[]{:S(2)}, u32[]{:S(2)}) collective-permute-start(f32[1,8,32,1024]{3,2,1,0:T(8,128)S(1)} %constant_dynamic-update-slice_fusion.16), channel_id=1, source_target_pairs={{0,16},{8,24},{16,0},{24,8},{32,48},{40,56},{48,32},{56,40},{64,80... | collective-permute-start | bytes 3145736 | tf_op jit(solution)/shard_map/ppermute | solution.py:13
  693.6 9.7 collective-permute-start.35
  734.7 9.6 collective-permute-start.44
  744.5 22.6 %collective-permute-start.45 = (f32[1,8,32,1024]{3,2,1,0:T(8,128)S(1)}, f32[1,8,32,1024]{3,2,1,0:T(8,128)S(1)}, u32[]{:S(2)}, u32[]{:S(2)}) collective-permute-start(f32[1,8,32,1024]{3,2,1,0:T(8,128)S(1)} %maximum_select_fusion.11), channel_id=1, source_target_pairs={{0,16},{8,24},{16,0},{24,8},{32,48},{40,56},{48,32},{56,40},{64,80... | collective-permute-start | bytes 3145736 | tf_op jit(solution)/shard_map/ppermute | solution.py:13
  767.3 11.1 collective-permute-start.46
  1090.6 13.4 %collective-permute-start.54 = (f32[1,8,16,1024]{3,2,1,0:T(8,128)}, f32[1,8,16,1024]{3,2,1,0:T(8,128)}, u32[]{:S(2)}, u32[]{:S(2)}) collective-permute-start(f32[1,8,16,1024]{3,2,1,0:T(8,128)} %constant_dynamic-update-slice_fusion), channel_id=1, source_target_pairs={{0,32},{8,40},{16,48},{24,56},{32,0},{40,8},{48,16},{56,24},{64,96... | collective-permute-start | bytes 1572872 | tf_op jit(solution)/shard_map/ppermute | solution.py:13
  1106.7 19.7 %collective-permute-start.55 = (f32[1,8,32,1024]{3,2,1,0:T(8,128)}, f32[1,8,32,1024]{3,2,1,0:T(8,128)}, u32[]{:S(2)}, u32[]{:S(2)}) collective-permute-start(f32[1,8,32,1024]{3,2,1,0:T(8,128)} %maximum_select_fusion.13), channel_id=1, source_target_pairs={{0,16},{8,24},{16,0},{24,8},{32,48},{40,56},{48,32},{56,40},{64,80... | collective-permute-start | bytes 3145736 | tf_op jit(solution)/shard_map/ppermute | solution.py:13
  1129.8 22.3 %collective-permute-start.56 = (f32[1,8,64,1024]{3,2,1,0:T(8,128)}, f32[1,8,64,1024]{3,2,1,0:T(8,128)}, u32[]{:S(2)}, u32[]{:S(2)}) collective-permute-start(f32[1,8,64,1024]{3,2,1,0:T(8,128)} %maximum_select_fusion.9), channel_id=1, source_target_pairs={{0,8},{8,0},{16,24},{24,16},{32,40},{40,32},{48,56},{56,48},{64,72... | collective-permute-start | bytes 6291464 | tf_op jit(solution)/shard_map/ppermute | solution.py:13
  (136 other events, 2283.8 us)
